TPU v7x, 512 devices: a whole 4x8x8 slice. The times are simulated.
512 devices in a mesh: grp: 4 (over y_lo, core), src: 16 (over y_hi, x), rcv: 8 (over z).
Axes of the slice: x: 4, y: 8 (y_hi: 4, y_lo: 2; y = y_hi * 2 + y_lo), z: 8, core: 2. Of those that a mesh axis runs over, the one named last changes fastest.
Arguments:
- recorded: bfloat16 [4, 2, 4096, 4096], P('grp', None, 'src', 'rcv'), parts along dimension 0, as said below
- aperture: int32 [128, 32, 3], P(('grp', 'src'), 'rcv'), parts along dimension 0, may hold values from 0 to 32, as said below
Outputs:
- multiples: float32 [4, 2, 4096, 4096], P('grp', None, 'src', 'rcv'), parts along dimension 0
There are 4 independent parts, one for each index of `grp`. A program takes and returns all parts, laid end to end along the dimension named above; each array names one. Nothing has to cross between parts.
Inputs may be any that keep to these rules, and one draw needn't show every extreme that they name: The data obey reciprocity: recorded(f, c, q, j) equals recorded(f, c, j, q). `aperture`: field 1 is from 4 to 32, field 0 plus field 1 is at most 32, field 2 is from 0 to 2. In every draw some tile pair spans all 32 k-blocks and some has taper width 2.
All inputs are finite; a program needn't handle non-finite values.
Results may differ from a plain program's by a relative error of at most 0.0004.
Values may be sent and summed in bfloat16 or wider, within the bound.
No kernel may reach another device: no remote copies, remote signals or barrier semaphores. Data moves between devices by JAX's collectives and lax.ppermute only.
A program may use at most 64 MiB of HBM per device.

v0:
```python
import jax
import jax.numpy as jnp
from jax import lax
from jax.sharding import PartitionSpec as P

NB = 32
TILE = 128


def tile_weights(aperture):
    block_ids = jnp.arange(NB, dtype=jnp.int32)
    offset = block_ids[None, None, :] - aperture[..., 0:1]
    extent = aperture[..., 1:2]
    taper_width = aperture[..., 2:3]
    margin = jnp.minimum(offset, extent - 1 - offset)
    ramped = jnp.minimum(
        1.0, (margin + 1).astype(jnp.float32) / (taper_width + 1).astype(jnp.float32)
    )
    return jnp.where((offset >= 0) & (offset < extent), ramped, 0.0)


def shards(recorded, aperture):
    slices = recorded.shape[0]
    own_rows = recorded.shape[2]
    own_cols = recorded.shape[3]
    row_tiles = own_rows // TILE
    col_tiles = own_cols // TILE
    weights = tile_weights(aperture)
    block_ids = jnp.arange(NB, dtype=jnp.int32)
    left_panel = lax.all_gather(recorded, "rcv", axis=3, tiled=True)

    def block_terms(incoming, first_row, span_rows, tile_weight):
        part_left = lax.dynamic_slice_in_dim(left_panel, first_row, span_rows, 3)
        part_left = part_left.reshape(slices, 2, row_tiles, TILE, span_rows)
        block_of = (first_row + jnp.arange(span_rows, dtype=jnp.int32)) // TILE
        row_weights = jnp.sum(
            jnp.where(block_of[:, None] == block_ids[None, :], tile_weight[:, :, None, :], 0.0),
            axis=-1,
        )
        scaled = (part_left[:, :, :, None, :, :] * row_weights[None, None, :, :, None, :]).astype(
            jnp.bfloat16
        )
        sub_tiles = tile_weight.shape[1]
        right_tiles = incoming.reshape(slices, 2, span_rows, sub_tiles, TILE)
        products = jnp.einsum(
            "fastik,fbktj->fabstij", scaled, right_tiles, preferred_element_type=jnp.float32
        )
        return jnp.stack(
            [products[:, 0, 0] - products[:, 1, 1], products[:, 0, 1] + products[:, 1, 0]], 1
        )

    empty = jnp.zeros((slices, 2, row_tiles, col_tiles, TILE, TILE), jnp.float32)
    incoming = lax.all_gather(recorded, "src", axis=2, tiled=True)
    extent = incoming.shape[2]

    def add_block(first_row, span_rows, running):
        portion = lax.dynamic_slice_in_dim(incoming, first_row, span_rows, 2)
        return running + block_terms(portion, first_row, span_rows, weights)

    sweeps = extent // TILE
    summed = lax.fori_loop(
        0, sweeps, lambda number, running: add_block(number * TILE, TILE, running), empty
    )
    return summed.transpose(0, 1, 2, 4, 3, 5).reshape(slices, 2, own_rows, own_cols)


def solution(mesh):
    in_specs = (P("grp", None, "src", "rcv"), P(("grp", "src"), "rcv", None))
    out_specs = P("grp", None, "src", "rcv")
    return jax.shard_map(shards, mesh=mesh, in_specs=in_specs, out_specs=out_specs, check_vma=False)
```

profile of v0, /device:TPU:1, one launch (start us, length us, event | category | flops | bytes accessed | tf_op | source)
XLA Modules:
  0.0 312.6 jit_solution(3568070417147690657)
XLA Ops:
  7.3 2.0 copy.15
  10.1 63.1 %all-gather.5.cloned.1.call-done = bf16[1,2,256,4096]{3,2,1,0:T(8,128)(2,1)} async-done(((bf16[1,2,256,512]{3,2,1,0:T(8,128)(2,1)}), bf16[1,2,256,4096]{3,2,1,0:T(8,128)(2,1)}) %all-gather.5.cloned.1.call-update) | async-done | bytes 4194320 | tf_op jit(solution)/shard_map/all_gather | solution.py:30
  73.2 131.2 %all-gather.3.cloned.1.call-done = bf16[1,2,4096,512]{2,3,1,0:T(8,128)(2,1)} async-done(((bf16[1,2,256,512]{2,3,1,0:T(8,128)(2,1)}), bf16[1,2,4096,512]{2,3,1,0:T(8,128)(2,1)}) %all-gather.3.cloned.1.call-update) | async-done | bytes 8388624 | tf_op jit(solution)/shard_map/all_gather | solution.py:53
  204.4 99.5 %while.16 = (s32[]{:T(128)}, f32[1,2,2,4,128,128]{4,5,2,3,1,0:T(8,128)S(1)}, bf16[1,2,4096,512]{2,3,1,0:T(8,128)(2,1)}, bf16[1,2,256,4096]{3,2,1,0:T(8,128)(2,1)...) while((s32[]{:T(128)}, ...), condition=%wide.region_2.3_spmd.clone, body=%wide.region_0.2_spmd.clone.sunk | while | flops 135929600 | bytes 10120505 | solution.py:61
  205.4 1.0 constant_dynamic-slice_fusion.5
  207.5 0.9 constant_dynamic-slice_fusion.4
  208.5 1.0 constant_dynamic-slice_fusion.5
  210.6 0.9 constant_dynamic-slice_fusion.4
  211.6 1.0 constant_dynamic-slice_fusion.5
  213.7 0.9 constant_dynamic-slice_fusion.4
  214.7 1.0 constant_dynamic-slice_fusion.5
  216.8 0.9 constant_dynamic-slice_fusion.4
  217.8 1.0 constant_dynamic-slice_fusion.5
  220.0 0.9 constant_dynamic-slice_fusion.4
  220.9 1.0 constant_dynamic-slice_fusion.5
  223.1 0.9 constant_dynamic-slice_fusion.4
  224.0 1.0 constant_dynamic-slice_fusion.5
  226.2 0.9 constant_dynamic-slice_fusion.4
  227.1 1.0 constant_dynamic-slice_fusion.5
  230.2 1.0 constant_dynamic-slice_fusion.5
  232.4 0.9 constant_dynamic-slice_fusion.4
  233.4 1.0 constant_dynamic-slice_fusion.5
  236.5 1.0 constant_dynamic-slice_fusion.5
  239.6 1.0 constant_dynamic-slice_fusion.5
  242.7 1.0 constant_dynamic-slice_fusion.5
  245.8 1.0 constant_dynamic-slice_fusion.5
  248.0 0.9 constant_dynamic-slice_fusion.4
  248.9 1.0 constant_dynamic-slice_fusion.5
  252.0 1.0 constant_dynamic-slice_fusion.5
  254.2 0.9 constant_dynamic-slice_fusion.4
  255.1 1.0 constant_dynamic-slice_fusion.5
  257.3 0.9 constant_dynamic-slice_fusion.4
  258.3 1.0 constant_dynamic-slice_fusion.5
  261.4 1.0 constant_dynamic-slice_fusion.5
  264.5 1.0 constant_dynamic-slice_fusion.5
  267.6 1.0 constant_dynamic-slice_fusion.5
  270.7 1.0 constant_dynamic-slice_fusion.5
  273.8 1.0 constant_dynamic-slice_fusion.5
  276.9 1.0 constant_dynamic-slice_fusion.5
  280.0 1.0 constant_dynamic-slice_fusion.5
  283.1 1.0 constant_dynamic-slice_fusion.5
  286.3 1.0 constant_dynamic-slice_fusion.5
  289.4 1.0 constant_dynamic-slice_fusion.5
  292.5 1.0 constant_dynamic-slice_fusion.5
  295.6 1.0 constant_dynamic-slice_fusion.5
  298.7 1.0 constant_dynamic-slice_fusion.5
  301.8 1.0 constant_dynamic-slice_fusion.5
  304.4 1.4 reshape.136
  (348 shorter events, 57.1 us)
Async XLA Ops:
  6.5 66.7 %all-gather.5.cloned.1.call-start = ((), (), s32[]{:S(2)}) async-start(), calls=%async_computation.1 | async-start | bytes 4718592 | tf_op jit(solution)/shard_map/all_gather | solution.py:30
  7.3 197.1 %all-gather.3.cloned.1.call-start = ((), (), s32[]{:S(2)}) async-start(), calls=%async_computation | async-start | bytes 8912896 | tf_op jit(solution)/shard_map/all_gather | solution.py:53
Sparse Core Ops, SparseCore 0:
  9.4 63.7 all-gather.4
  76.2 128.1 all-gather.2
where the time goes:
time: 314 us; the launch traced here: 313 us
  waiting for transfers between devices  195 us (62%)
  local copies, waits for them, and re-layouts  64.6 us (21%)
  other arithmetic  22.6 us (7%)
  matrix products  13.9 us (4%)
  between operations  13.4 us (4%)
    all_gather x1, waiting for transfers between devices, shards(): incoming = lax.all_gather(recorded, 'src', axis=2, tiled=True)  131 us
    all_gather x1, waiting for transfers between devices, shards(): left_panel = lax.all_gather(recorded, 'rcv', axis=3, tiled=True)  63.1 us
    dynamic_slice x32, local copies, waits for them, and re-layouts, add_block(): portion = lax.dynamic_slice_in_dim(incoming, first_row, span_rows, 2)  31.2 us
    dynamic_slice x32, local copies, waits for them, and re-layouts, block_terms(): part_left = lax.dynamic_slice_in_dim(left_panel, first_row, span_rows, 3)  29.4 us
    dot_general x32, matrix products, block_terms(): jnp.einsum('fastik,fbktj->fabstij', scaled, right_tiles, preferred_elemen...  13.9 us
    add x32, other arithmetic, add_block(): return running + block_terms(portion, first_row, span_rows, weights)  10.7 us
  transfers between devices with their start and end apart: 2, of which 2 were waited for; matrix products, arithmetic and copies ran while one was open for 1% of the time, Pallas kernels for 0%

commit v1 on v0

--- a/solution.py
+++ b/solution.py
@@ -5,6 +5,27 @@
 
 NB = 32
 TILE = 128
+
+
+def ring_gather(shard, axis, dim):
+    count, mine, rows = (lax.axis_size(axis), lax.axis_index(axis), shard.shape[dim])
+    upward = [(i, (i + 1) % count) for i in range(count)]
+    backward = [(i, (i - 1) % count) for i in range(count)]
+    result = jnp.zeros((*shard.shape[:dim], count * rows, *shard.shape[dim + 1 :]), shard.dtype)
+    result = lax.dynamic_update_slice_in_dim(result, shard, mine * rows, axis=dim)
+    from_left = from_right = shard
+    middle = count // 2
+    for step in range(1, middle + 1):
+        from_left = lax.ppermute(from_left, axis, upward)
+        result = lax.dynamic_update_slice_in_dim(
+            result, from_left, (mine - step) % count * rows, axis=dim
+        )
+        if step < count - middle:
+            from_right = lax.ppermute(from_right, axis, backward)
+            result = lax.dynamic_update_slice_in_dim(
+                result, from_right, (mine + step) % count * rows, axis=dim
+            )
+    return result
 
 
 def tile_weights(aperture):
@@ -27,7 +48,7 @@
     col_tiles = own_cols // TILE
     weights = tile_weights(aperture)
     block_ids = jnp.arange(NB, dtype=jnp.int32)
-    left_panel = lax.all_gather(recorded, "rcv", axis=3, tiled=True)
+    left_panel = ring_gather(recorded, "rcv", 3)
 
     def block_terms(incoming, first_row, span_rows, tile_weight):
         part_left = lax.dynamic_slice_in_dim(left_panel, first_row, span_rows, 3)

time: 314 us -> 256 us (0.82)
  waiting for transfers between devices: 195 us -> 98.1 us
  starting transfers between devices: 0.04 us -> 28.4 us
  local copies, waits for them, and re-layouts: 64.6 us -> 75.2 us
    all_gather x1 -> x0, waiting for transfers between devices: 63.1 us -> none  [shards(): left_panel = lax.all_gather(recorded, 'rcv', axis=3, tiled=True)]
    all_gather x1, waiting for transfers between devices: 131 us -> 69.5 us  [shards(): incoming = lax.all_gather(recorded, 'src', axis=2, tiled=True)]
    ppermute x0 -> x7, waiting for transfers between devices: none -> 28.6 us  [the longest x4 28.6 us: ring_gather(): from_left = lax.ppermute(from_left, axis, upward)]
    ppermute x0 -> x7, starting transfers between devices: none -> 28.4 us  [the longest x3 17.8 us: ring_gather(): from_right = lax.ppermute(from_right, axis, backward)]
    dynamic_update_slice x0 -> x8, local copies, waits for them, and re-layouts: none -> 8.05 us  [the longest x4 4.63 us: ring_gather(): lax.dynamic_update_slice_in_dim(result, from_left, (mine - step) % count...]
  transfers between devices with their start and end apart: 2 -> 8, of which waited for: 2 -> 5; matrix products, arithmetic and copies ran while one was open for 1% -> 4% of each run, Pallas kernels for 0% -> 0%
where the time goes in v1:
time: 256 us; the launch traced here: 254 us
  waiting for transfers between devices  98.1 us (38%)
  local copies, waits for them, and re-layouts  75.2 us (29%)
  starting transfers between devices  28.4 us (11%)
  other arithmetic  21.9 us (9%)
  matrix products  13.9 us (5%)
  between operations  13.7 us (5%)
  loops' own time  2.99 us (1%)
    all_gather x1, waiting for transfers between devices, shards(): incoming = lax.all_gather(recorded, 'src', axis=2, tiled=True)  69.5 us
    dynamic_slice x32, local copies, waits for them, and re-layouts, add_block(): portion = lax.dynamic_slice_in_dim(incoming, first_row, span_rows, 2)  31.2 us
    dynamic_slice x32, local copies, waits for them, and re-layouts, block_terms(): part_left = lax.dynamic_slice_in_dim(left_panel, first_row, span_rows, 3)  29.4 us
    ppermute x4, waiting for transfers between devices, ring_gather(): from_left = lax.ppermute(from_left, axis, upward)  28.6 us
    ppermute x3, starting transfers between devices, ring_gather(): from_right = lax.ppermute(from_right, axis, backward)  17.8 us
    dot_general x32, matrix products, block_terms(): jnp.einsum('fastik,fbktj->fabstij', scaled, right_tiles, preferred_elemen...  13.9 us
    add x32, other arithmetic, add_block(): return running + block_terms(portion, first_row, span_rows, weights)  10.7 us
    ppermute x4, starting transfers between devices, ring_gather(): from_left = lax.ppermute(from_left, axis, upward)  10.6 us
  transfers between devices with their start and end apart: 8, of which 5 were waited for; matrix products, arithmetic and copies ran while one was open for 4% of the time, Pallas kernels for 0%

profile of v1, /device:TPU:1, one launch (start us, length us, event | category | flops | bytes accessed | tf_op | source)
XLA Modules:
  0.0 254.2 jit_solution(6221283350488418075)
XLA Ops:
  6.5 2.1 copy.15
  8.7 4.8 %collective-permute-start = (bf16[1,2,256,512]{3,2,1,0:T(8,128)(2,1)}, bf16[1,2,256,512]{3,2,1,0:T(8,128)(2,1)S(1)}, u32[]{:S(2)}, u32[]{:S(2)}) collective-permute-start(bf16[1,2,256,512]{3,2,1,0:T(8,128)(2,1)} %param.4), channel_id=1, source_target_pairs={{0,1},{1,2},{2,3},{3,4},{4,5},{5,6},{6,7},{7,0},{8,9},{9,10},{10,1... | collective-permute-start | bytes 1572872 | tf_op jit(solution)/shard_map/ppermute | solution.py:19
  13.5 8.6 %collective-permute-start.1 = (bf16[1,2,256,512]{3,2,1,0:T(8,128)(2,1)}, bf16[1,2,256,512]{3,2,1,0:T(8,128)(2,1)S(1)}, u32[]{:S(2)}, u32[]{:S(2)}) collective-permute-start(bf16[1,2,256,512]{3,2,1,0:T(8,128)(2,1)} %param.4), channel_id=1, source_target_pairs={{0,7},{1,0},{2,1},{3,2},{4,3},{5,4},{6,5},{7,6},{8,15},{9,8},{10,9... | collective-permute-start | bytes 1572872 | tf_op jit(solution)/shard_map/ppermute | solution.py:24
  22.1 9.9 %collective-permute-done = bf16[1,2,256,512]{3,2,1,0:T(8,128)(2,1)S(1)} collective-permute-done((bf16[1,2,256,512]{3,2,1,0:T(8,128)(2,1)}, bf16[1,2,256,512]{3,2,1,0:T(8,128)(2,1)S(1)}, u32[]{:S(2)}, u32[]{:S(2)}) %collective-permute-start) | collective-permute-done | bytes 524320 | tf_op jit(solution)/shard_map/ppermute | solution.py:19
  32.0 1.9 collective-permute-start.2
  34.0 4.6 %collective-permute-start.3 = (bf16[1,2,256,512]{3,2,1,0:T(8,128)(2,1)S(1)}, bf16[1,2,256,512]{3,2,1,0:T(8,128)(2,1)S(1)}, u32[]{:S(2)}, u32[]{:S(2)}) collective-permute-start(bf16[1,2,256,512]{3,2,1,0:T(8,128)(2,1)S(1)} %collective-permute-done.1), channel_id=1, source_target_pairs={{0,7},{1,0},{2,1},{3,2},{4,3},{5,4},{6,5},{7,6},{8,15},{9,8},{10,9... | collective-permute-start | bytes 1572872 | tf_op jit(solution)/shard_map/ppermute | solution.py:24
  38.5 8.9 %collective-permute-done.2 = bf16[1,2,256,512]{3,2,1,0:T(8,128)(2,1)} collective-permute-done((bf16[1,2,256,512]{3,2,1,0:T(8,128)(2,1)S(1)}, bf16[1,2,256,512]{3,2,1,0:T(8,128)(2,1)}, u32[]{:S(2)}, u32[]{:S(2)}) %collective-permute-start.2) | collective-permute-done | bytes 524320 | tf_op jit(solution)/shard_map/ppermute | solution.py:19
  47.4 1.9 collective-permute-start.4
  49.5 2.5 broadcast_in_dim.65
  52.9 4.6 %collective-permute-start.5 = (bf16[1,2,256,512]{3,2,1,0:T(8,128)(2,1)S(1)}, bf16[1,2,256,512]{3,2,1,0:T(8,128)(2,1)S(1)}, u32[]{:S(2)}, u32[]{:S(2)}) collective-permute-start(bf16[1,2,256,512]{3,2,1,0:T(8,128)(2,1)S(1)} %collective-permute-done.3), channel_id=1, source_target_pairs={{0,7},{1,0},{2,1},{3,2},{4,3},{5,4},{6,5},{7,6},{8,15},{9,8},{10,9... | collective-permute-start | bytes 1572872 | tf_op jit(solution)/shard_map/ppermute | solution.py:24
  58.5 3.5 %collective-permute-done.4 = bf16[1,2,256,512]{3,2,1,0:T(8,128)(2,1)S(1)} collective-permute-done((bf16[1,2,256,512]{3,2,1,0:T(8,128)(2,1)}, bf16[1,2,256,512]{3,2,1,0:T(8,128)(2,1)S(1)}, u32[]{:S(2)}, u32[]{:S(2)}) %collective-permute-start.4) | collective-permute-done | bytes 524320 | tf_op jit(solution)/shard_map/ppermute | solution.py:19
  62.0 1.9 collective-permute-start.6
  64.8 1.9 constant_dynamic-update-slice_fusion.4
  69.3 6.2 %collective-permute-done.6 = bf16[1,2,256,512]{3,2,1,0:T(8,128)(2,1)S(1)} collective-permute-done((bf16[1,2,256,512]{3,2,1,0:T(8,128)(2,1)S(1)}, bf16[1,2,256,512]{3,2,1,0:T(8,128)(2,1)S(1)}, u32[]{:S(2)}, u32[]{:S(2)}) %collective-permute-start.6) | collective-permute-done | bytes 524320 | tf_op jit(solution)/shard_map/ppermute | solution.py:19
  76.4 69.5 %all-gather.2.cloned.1.call-done = bf16[1,2,4096,512]{2,3,1,0:T(8,128)(2,1)} async-done(((bf16[1,2,256,512]{2,3,1,0:T(8,128)(2,1)}), bf16[1,2,4096,512]{2,3,1,0:T(8,128)(2,1)}) %all-gather.2.cloned.1.call-update) | async-done | bytes 8388624 | tf_op jit(solution)/shard_map/all_gather | solution.py:74
  146.0 99.6 %while.16 = (s32[]{:T(128)}, f32[1,2,2,4,128,128]{4,5,2,3,1,0:T(8,128)S(1)}, bf16[1,2,4096,512]{2,3,1,0:T(8,128)(2,1)}, bf16[1,2,256,4096]{3,2,1,0:T(8,128)(2,1)...) while((s32[]{:T(128)}, ...), condition=%wide.region_2.3_spmd.clone, body=%wide.region_0.2_spmd.clone.sunk | while | flops 135929600 | bytes 10120505 | solution.py:82
  146.9 1.0 constant_dynamic-slice_fusion.5
  150.0 1.0 constant_dynamic-slice_fusion.5
  153.1 1.0 constant_dynamic-slice_fusion.5
  156.3 1.0 constant_dynamic-slice_fusion.5
  159.4 1.0 constant_dynamic-slice_fusion.5
  162.5 1.0 constant_dynamic-slice_fusion.5
  165.6 1.0 constant_dynamic-slice_fusion.5
  168.7 1.0 constant_dynamic-slice_fusion.5
  171.8 1.0 constant_dynamic-slice_fusion.5
  174.9 1.0 constant_dynamic-slice_fusion.5
  178.0 1.0 constant_dynamic-slice_fusion.5
  181.1 1.0 constant_dynamic-slice_fusion.5
  184.3 1.0 constant_dynamic-slice_fusion.5
  187.4 1.0 constant_dynamic-slice_fusion.5
  190.5 1.0 constant_dynamic-slice_fusion.5
  193.6 1.0 constant_dynamic-slice_fusion.5
  196.7 1.0 constant_dynamic-slice_fusion.5
  199.8 1.0 constant_dynamic-slice_fusion.5
  202.9 1.0 constant_dynamic-slice_fusion.5
  206.0 1.0 constant_dynamic-slice_fusion.5
  209.2 1.0 constant_dynamic-slice_fusion.5
  212.3 1.0 constant_dynamic-slice_fusion.5
  215.4 1.0 constant_dynamic-slice_fusion.5
  218.5 1.0 constant_dynamic-slice_fusion.5
  221.6 1.0 constant_dynamic-slice_fusion.5
  224.7 1.0 constant_dynamic-slice_fusion.5
  227.8 1.0 constant_dynamic-slice_fusion.5
  230.9 1.0 constant_dynamic-slice_fusion.5
  237.2 1.0 constant_dynamic-slice_fusion.5
  240.3 1.0 constant_dynamic-slice_fusion.5
  243.4 1.0 constant_dynamic-slice_fusion.5
  245.9 1.4 reshape.136
  (376 shorter events, 72.9 us)
Async XLA Ops:
  6.5 45.5 %copy-start = (bf16[1,2,256,512]{3,2,1,0:T(8,128)(2,1)S(1)}, bf16[1,2,256,512]{3,2,1,0:T(8,128)(2,1)}, u32[]{:S(2)}) copy-start(bf16[1,2,256,512]{3,2,1,0:T(8,128)(2,1)} %param.4) | copy-start | bytes 1572868
  6.5 46.3 %copy-start.3 = (s32[2,4,3]{1,0,2:T(2,128)S(1)}, s32[2,4,3]{1,0,2:T(2,128)}, u32[]{:S(2)}) copy-start(s32[2,4,3]{1,0,2:T(2,128)} %param.5) | copy-start | bytes 292
  6.5 139.4 %all-gather.2.cloned.1.call-start = ((), (), s32[]{:S(2)}) async-start(), calls=%async_computation | async-start | bytes 8912896 | tf_op jit(solution)/shard_map/all_gather | solution.py:74
  8.7 23.4 %collective-permute-start = (bf16[1,2,256,512]{3,2,1,0:T(8,128)(2,1)}, bf16[1,2,256,512]{3,2,1,0:T(8,128)(2,1)S(1)}, u32[]{:S(2)}, u32[]{:S(2)}) collective-permute-start(bf16[1,2,256,512]{3,2,1,0:T(8,128)(2,1)} %param.4), channel_id=1, source_target_pairs={{0,1},{1,2},{2,3},{3,4},{4,5},{5,6},{6,7},{7,0},{8,9},{9,10},{10,1... | collective-permute-start | bytes 1572872 | tf_op jit(solution)/shard_map/ppermute | solution.py:19
  13.5 20.4 %collective-permute-start.1 = (bf16[1,2,256,512]{3,2,1,0:T(8,128)(2,1)}, bf16[1,2,256,512]{3,2,1,0:T(8,128)(2,1)S(1)}, u32[]{:S(2)}, u32[]{:S(2)}) collective-permute-start(bf16[1,2,256,512]{3,2,1,0:T(8,128)(2,1)} %param.4), channel_id=1, source_target_pairs={{0,7},{1,0},{2,1},{3,2},{4,3},{5,4},{6,5},{7,6},{8,15},{9,8},{10,9... | collective-permute-start | bytes 1572872 | tf_op jit(solution)/shard_map/ppermute | solution.py:24
  32.0 17.4 %copy-start.1 = (bf16[1,2,256,512]{3,2,1,0:T(8,128)(2,1)}, bf16[1,2,256,512]{3,2,1,0:T(8,128)(2,1)S(1)}, u32[]{:S(2)}) copy-start(bf16[1,2,256,512]{3,2,1,0:T(8,128)(2,1)S(1)} %collective-permute-done) | copy-start | bytes 1572868
  32.0 15.4 %collective-permute-start.2 = (bf16[1,2,256,512]{3,2,1,0:T(8,128)(2,1)S(1)}, bf16[1,2,256,512]{3,2,1,0:T(8,128)(2,1)}, u32[]{:S(2)}, u32[]{:S(2)}) collective-permute-start(bf16[1,2,256,512]{3,2,1,0:T(8,128)(2,1)S(1)} %collective-permute-done), channel_id=1, source_target_pairs={{0,1},{1,2},{2,3},{3,4},{4,5},{5,6},{6,7},{7,0},{8,9},{9,10},{10,1... | collective-permute-start | bytes 1572872 | tf_op jit(solution)/shard_map/ppermute | solution.py:19
  34.0 18.9 %collective-permute-start.3 = (bf16[1,2,256,512]{3,2,1,0:T(8,128)(2,1)S(1)}, bf16[1,2,256,512]{3,2,1,0:T(8,128)(2,1)S(1)}, u32[]{:S(2)}, u32[]{:S(2)}) collective-permute-start(bf16[1,2,256,512]{3,2,1,0:T(8,128)(2,1)S(1)} %collective-permute-done.1), channel_id=1, source_target_pairs={{0,7},{1,0},{2,1},{3,2},{4,3},{5,4},{6,5},{7,6},{8,15},{9,8},{10,9... | collective-permute-start | bytes 1572872 | tf_op jit(solution)/shard_map/ppermute | solution.py:24
  47.4 14.6 %collective-permute-start.4 = (bf16[1,2,256,512]{3,2,1,0:T(8,128)(2,1)}, bf16[1,2,256,512]{3,2,1,0:T(8,128)(2,1)S(1)}, u32[]{:S(2)}, u32[]{:S(2)}) collective-permute-start(bf16[1,2,256,512]{3,2,1,0:T(8,128)(2,1)} %collective-permute-done.2), channel_id=1, source_target_pairs={{0,1},{1,2},{2,3},{3,4},{4,5},{5,6},{6,7},{7,0},{8,9},{9,10},{10,1... | collective-permute-start | bytes 1572872 | tf_op jit(solution)/shard_map/ppermute | solution.py:19
  49.5 8.0 %copy-start.2 = (bf16[1,2,256,512]{3,2,1,0:T(8,128)(2,1)S(1)}, bf16[1,2,256,512]{3,2,1,0:T(8,128)(2,1)}, u32[]{:S(2)}) copy-start(bf16[1,2,256,512]{3,2,1,0:T(8,128)(2,1)} %copy-done.1) | copy-start | bytes 1572868
  52.9 15.6 %collective-permute-start.5 = (bf16[1,2,256,512]{3,2,1,0:T(8,128)(2,1)S(1)}, bf16[1,2,256,512]{3,2,1,0:T(8,128)(2,1)S(1)}, u32[]{:S(2)}, u32[]{:S(2)}) collective-permute-start(bf16[1,2,256,512]{3,2,1,0:T(8,128)(2,1)S(1)} %collective-permute-done.3), channel_id=1, source_target_pairs={{0,7},{1,0},{2,1},{3,2},{4,3},{5,4},{6,5},{7,6},{8,15},{9,8},{10,9... | collective-permute-start | bytes 1572872 | tf_op jit(solution)/shard_map/ppermute | solution.py:24
  62.0 13.5 %collective-permute-start.6 = (bf16[1,2,256,512]{3,2,1,0:T(8,128)(2,1)S(1)}, bf16[1,2,256,512]{3,2,1,0:T(8,128)(2,1)S(1)}, u32[]{:S(2)}, u32[]{:S(2)}) collective-permute-start(bf16[1,2,256,512]{3,2,1,0:T(8,128)(2,1)S(1)} %collective-permute-done.4), channel_id=1, source_target_pairs={{0,1},{1,2},{2,3},{3,4},{4,5},{5,6},{6,7},{7,0},{8,9},{9,10},{10,1... | collective-permute-start | bytes 1572872 | tf_op jit(solution)/shard_map/ppermute | solution.py:19
Sparse Core Ops, SparseCore 0:
  10.3 135.5 all-gather.1
